TPU v7x, 512 devices: a whole 4x4x16 slice. The times are simulated.
512 devices in a mesh: dp: 64 (over z, y), owner: 8 (over x, core).
Axes of the slice: x: 4, y: 4, z: 16, core: 2. Of those that a mesh axis runs over, the one named last changes fastest.
Arguments:
- query_out: bfloat16 [512, 16384], P('dp', 'owner'), may hold values from -6 to 6
- query_in: bfloat16 [512, 8192], P('dp'), may hold values from -6 to 6
- train_out: bfloat16 [512, 16384], P('dp', 'owner'), may hold values from -6 to 6
- train_in: bfloat16 [512, 8192], P('dp'), may hold values from -6 to 6
- basis_out: bfloat16 [96, 256, 256], P('owner'), may hold values from -1 to 1, as said below
- basis_in: bfloat16 [64, 128, 128], P('dp'), may hold values from -1 to 1, as said below
- eigvals: float32 [24576, 8192], P('owner', 'dp'), may hold values from 0.1 to 10
- owner_map: int32 [64], replicated, may hold values from 0 to 7, as said below
Outputs:
- scores: float32 [8, 32], replicated
Inputs may be any that keep to these rules, and one draw needn't show every extreme that they name: owner_map[b] is the owner of hidden block b. Blocks form ranges of 8 in order; a block of range r is owned by r or by r xor 1. Of two such partner owners one holds exactly 12 blocks and keeps 12 // 2 of its own range, the other holds 4 blocks and keeps 8 - 12 // 2 of its own range. `basis_out`: each [256, 256] block is an orthogonal matrix rounded to bfloat16; block o * 12 + s belongs to the s-th block, in block order, that owner o holds; blocks past an owner's count are not read. `basis_in`: each [128, 128] block is an orthogonal matrix rounded to bfloat16.
All inputs are finite; a program needn't handle non-finite values.
Results may differ from a plain program's by a relative error of at most 0.0067.
Values may be sent and summed in bfloat16 or wider, within the bound.
No kernel may reach another device: no remote copies, remote signals or barrier semaphores. Data moves between devices by JAX's collectives and lax.ppermute only.
A program may use at most 64 MiB of HBM per device.

v0:
```python
import math
import jax
import jax.numpy as jnp
from jax import lax
from jax.sharding import PartitionSpec as P

NQ = 8
ET = 16
DAMPING = 0.1


def from_partner(array, axis, stride):
    return lax.ppermute(array, axis, [(i, i ^ 1 << stride) for i in range(lax.axis_size(axis))])


def slot_tables(owner_map, owner_index, blocks_own, capacity):
    pair_count = 2 * blocks_own
    pair_base = owner_index // 2 * pair_count
    pair_owner = lax.dynamic_slice_in_dim(owner_map, pair_base, pair_count)
    owned_mask = (pair_owner == owner_index).astype(jnp.int32)
    slot_rank = jnp.cumsum(owned_mask) - 1
    slot_ids = jnp.arange(capacity, dtype=jnp.int32)
    pair_hot = (owned_mask[:, None] == 1) & (slot_rank[:, None] == slot_ids[None, :])
    own_start = owner_index % 2 * blocks_own
    other_start = blocks_own - own_start
    keep_hot = lax.dynamic_slice_in_dim(pair_hot, own_start, blocks_own, 0)
    other_hot = lax.dynamic_slice_in_dim(pair_hot, other_start, blocks_own, 0)
    send_ids = jnp.arange(capacity // 2, dtype=jnp.int32)
    from_other = lax.dynamic_slice_in_dim(owned_mask, other_start, blocks_own)
    other_rank = jnp.cumsum(from_other) - 1
    arrive_hot = (from_other[:, None] == 1) & (other_rank[:, None] == send_ids[None, :])
    arrive_slot = jnp.dot(arrive_hot.T.astype(jnp.float32), other_hot.astype(jnp.float32))
    to_other = 1 - lax.dynamic_slice_in_dim(owned_mask, own_start, blocks_own)
    depart_rank = jnp.cumsum(to_other) - 1
    depart_hot = (to_other[:, None] == 1) & (depart_rank[:, None] == send_ids[None, :])
    return (
        keep_hot.astype(jnp.bfloat16),
        depart_hot.astype(jnp.bfloat16),
        arrive_slot.astype(jnp.bfloat16),
    )


def departing(tokens, depart_hot, block_width):
    blocks = tokens.reshape(tokens.shape[0], -1, block_width)
    return jnp.einsum("rpk,ps->rsk", blocks, depart_hot, preferred_element_type=jnp.float32).astype(
        jnp.bfloat16
    )


def to_slots(tokens, arrived, keep_hot, arrive_slot, block_width):
    blocks = tokens.reshape(tokens.shape[0], -1, block_width)
    kept_part = jnp.einsum("rpk,pc->rck", blocks, keep_hot, preferred_element_type=jnp.float32)
    moved_part = jnp.einsum("rsk,sc->rck", arrived, arrive_slot, preferred_element_type=jnp.float32)
    return (kept_part + moved_part).astype(jnp.bfloat16)


def rotate_outputs(slotted, basis_out):
    return jnp.einsum(
        "rck,ckl->rcl", slotted, basis_out, preferred_element_type=jnp.float32
    ).astype(jnp.bfloat16)


def rotate_inputs(columns_local, basis_in):
    token_count = columns_local.shape[0]
    blocks = columns_local.reshape(token_count, basis_in.shape[0], basis_in.shape[1])
    turned = jnp.einsum("tnb,nbc->tnc", blocks, basis_in, preferred_element_type=jnp.float32)
    return turned.astype(jnp.bfloat16).reshape(token_count, -1)


def condition(query_rot, query_act, eigvals, basis_in, basis_out):
    capacity, block_width = (basis_out.shape[0], basis_out.shape[1])
    in_blocks, in_width = (basis_in.shape[0], basis_in.shape[1])
    per_query = query_rot.shape[0] // NQ
    query_flat = query_rot.reshape(query_rot.shape[0], capacity * block_width)
    shifted = eigvals + DAMPING
    results = []
    for query_index in range(NQ):
        left_side = query_flat[query_index * per_query : (query_index + 1) * per_query]
        right_side = query_act[query_index * per_query : (query_index + 1) * per_query]
        moment = lax.dot_general(
            left_side, right_side, (((0,), (0,)), ((), ())), preferred_element_type=jnp.float32
        )
        damped = (moment / shifted).astype(jnp.bfloat16)
        half_back = jnp.einsum(
            "fnb,ncb->fnc",
            damped.reshape(-1, in_blocks, in_width),
            basis_in,
            preferred_element_type=jnp.float32,
        ).astype(jnp.bfloat16)
        restored = jnp.einsum(
            "ckl,cld->ckd",
            basis_out,
            half_back.reshape(capacity, block_width, -1),
            preferred_element_type=jnp.float32,
        ).astype(jnp.bfloat16)
        results.append(restored.reshape(capacity * block_width, -1))
    return jnp.stack(results)


def score_tokens(precond, train_slots, train_inputs, example_count):
    projected = jnp.einsum("tf,qfd->qtd", train_slots, precond, preferred_element_type=jnp.float32)
    per_token = jnp.sum(projected * train_inputs.astype(jnp.float32)[None], axis=2)
    token_ids = jnp.arange(train_slots.shape[0], dtype=jnp.int32)
    example_hot = (
        token_ids[:, None] // ET == jnp.arange(example_count, dtype=jnp.int32)[None, :]
    ).astype(jnp.float32)
    return jnp.dot(per_token, example_hot, precision=lax.Precision.HIGHEST)


def local(query_out, query_in, train_out, train_in, basis_out, basis_in, eigvals, owner_map):
    owner_index = lax.axis_index("owner")
    capacity = basis_out.shape[0]
    block_width = basis_out.shape[1]
    blocks_own = query_out.shape[1] // block_width
    query_local = query_out.shape[0]
    keep_hot, depart_hot, arrive_slot = slot_tables(owner_map, owner_index, blocks_own, capacity)
    query_cols, train_cols = (
        lax.all_to_all(query_in, "dp", split_axis=1, concat_axis=0, tiled=True),
        lax.all_to_all(train_in, "dp", split_axis=1, concat_axis=0, tiled=True),
    )
    query_act = rotate_inputs(query_cols, basis_in)
    example_count = train_cols.shape[0] // ET
    local_tokens = jnp.concatenate([query_out, train_out], 0)
    leaving = departing(local_tokens, depart_hot, block_width)
    arrived = from_partner(leaving, "owner", 0)
    slotted = to_slots(local_tokens, arrived, keep_hot, arrive_slot, block_width)
    query_rot = rotate_outputs(slotted[:query_local], basis_out)
    train_local = slotted[query_local:]
    query_all = lax.all_gather(query_rot, "dp", axis=0, tiled=True)
    precond = condition(query_all, query_act, eigvals, basis_in, basis_out)
    piece_slots = lax.all_gather(train_local, "dp", axis=0, tiled=True)
    row_count = piece_slots.shape[0]
    partial_scores = score_tokens(
        precond, piece_slots.reshape(row_count, -1), train_cols, example_count
    )
    scores = lax.psum(partial_scores, ("dp", "owner"))
    per_query = query_act.shape[0] // NQ
    hidden_total = query_out.shape[1] * lax.axis_size("owner")
    score_scale = 1.0 / math.sqrt(per_query * ET * hidden_total * query_in.shape[1])
    return scores * score_scale


def solution(mesh):
    in_specs = (
        P("dp", "owner"),
        P("dp", None),
        P("dp", "owner"),
        P("dp", None),
        P("owner", None, None),
        P("dp", None, None),
        P("owner", "dp"),
        P(),
    )
    out_specs = P()
    return jax.shard_map(local, mesh=mesh, in_specs=in_specs, out_specs=out_specs, check_vma=False)
```

profile of v0, /device:TPU:1, one launch (start us, length us, event | category | flops | bytes accessed | tf_op | source)
XLA Modules:
  0.0 418.7 jit_solution(11607726487385089527)
XLA Ops:
  8.7 8.7 %collective-permute-start = (bf16[16,6,256]{2,1,0:T(8,128)(2,1)S(1)}, bf16[16,6,256]{2,1,0:T(8,128)(2,1)S(1)}, u32[]{:S(2)}, u32[]{:S(2)}) collective-permute-start(bf16[16,6,256]{2,1,0:T(8,128)(2,1)S(1)} %fusion.20), channel_id=1, source_target_pairs={{0,1},{1,0},{2,3},{3,2},{4,5},{5,4},{6,7},{7,6},{8,9},{9,8},{10,11... | collective-permute-start | bytes 147464 | tf_op jit(solution)/shard_map/ppermute | solution.py:13
  19.8 28.1 %all_to_all.29 = bf16[8,64,128]{2,0,1:T(8,128)(2,1)S(1)} all-to-all(bf16[8,64,128]{2,0,1:T(8,128)(2,1)S(1)} %bitcast.263), channel_id=1, replica_groups=mesh['dp'=64,'owner'=8] {'dp'}, dimensions={1} | all-to-all | bytes 262144 | tf_op jit(solution)/shard_map/all_to_all | solution.py:119
  47.9 6.4 %all-to-all-start = ((bf16[8,64,128]{2,0,1:T(8,128)(2,1)}), bf16[8,64,128]{2,0,1:T(8,128)(2,1)S(1)}, u32[]{:S(2)}, u32[]{:S(2)}) async-start(bf16[8,64,128]{2,0,1:T(8,128)(2,1)} %bitcast.12), calls=%async_computation | async-start | bytes 262144 | tf_op jit(solution)/shard_map/all_to_all | solution.py:118
  56.1 12.7 %all-to-all-done = bf16[8,64,128]{2,0,1:T(8,128)(2,1)S(1)} async-done(((bf16[8,64,128]{2,0,1:T(8,128)(2,1)}), bf16[8,64,128]{2,0,1:T(8,128)(2,1)S(1)}, u32[]{:S(2)}, u32[]{:S(2)}) %all-to-all-start) | async-done | bytes 131104 | tf_op jit(solution)/shard_map/all_to_all | solution.py:118
  69.7 80.6 %all-gather.3.cloned.1.call-done = bf16[512,12,256]{2,0,1:T(8,128)(2,1)} async-done(((bf16[8,12,256]{2,0,1:T(8,128)(2,1)}), bf16[512,12,256]{2,0,1:T(8,128)(2,1)}) %all-gather.3.cloned.1.call-update) | async-done | bytes 3145744 | tf_op jit(solution)/shard_map/all_gather | solution.py:129
  150.3 3.3 slice_bitcast_fusion
  153.6 2.1 convolution_convert_fusion.7
  157.1 1.0 copy.135
  158.1 3.1 convolution_convert_fusion.6
  161.2 1.8 fusion.10
  163.0 1.2 copy.93
  164.1 1.4 copy.113
  165.6 1.8 copy.136
  167.3 3.2 convolution_convert_fusion.5
  170.5 2.7 fusion.11
  173.2 2.3 copy.96
  175.5 2.3 copy.114
  177.7 1.8 copy.137
  179.6 3.2 convolution_convert_fusion.4
  182.8 2.7 fusion.12
  185.4 2.3 copy.99
  187.7 2.3 copy.115
  190.1 1.8 copy.138
  191.8 3.2 convolution_convert_fusion.3
  195.0 2.7 fusion.13
  197.7 2.3 copy.102
  200.0 2.3 copy.116
  202.3 1.8 copy.139
  204.1 3.2 convolution_convert_fusion.2
  207.3 2.7 fusion.14
  210.0 2.3 copy.105
  212.3 2.3 copy.117
  214.6 1.8 copy.140
  216.4 3.2 convolution_convert_fusion.1
  219.5 2.9 fusion.15
  222.4 2.3 copy.108
  224.7 2.4 copy.118
  227.9 3.2 convolution_convert_fusion
  231.1 2.7 fusion.16
  233.8 2.3 copy.111
  236.1 2.3 copy.119
  238.3 0.9 constant_dynamic-update-slice_fusion.7
  240.2 0.9 constant_dynamic-update-slice_fusion.5
  244.0 1.0 constant_dynamic-update-slice_fusion.1
  245.9 42.4 %all-gather.5.cloned.1.call-done = bf16[512,12,256]{2,0,1:T(8,128)(2,1)} async-done(((bf16[8,12,256]{2,0,1:T(8,128)(2,1)}), bf16[512,12,256]{2,0,1:T(8,128)(2,1)}) %all-gather.5.cloned.1.call-update) | async-done | bytes 3145744 | tf_op jit(solution)/shard_map/all_gather | solution.py:131
  288.4 4.7 %copy.121 = bf16[512,12,256]{0,2,1:T(8,128)(2,1)} copy(bf16[512,12,256]{2,0,1:T(8,128)(2,1)} %all-gather.5.cloned.1.call-done) | data formatting | bytes 6291456 | tf_op jit(solution)/shard_map/all_gather | solution.py:131
  293.1 7.1 %fusion.8 = f32[8,512]{1,0:T(8,128)S(1)} fusion(bf16[8,3072,128]{1,2,0:T(8,128)(2,1)} %constant_dynamic-update-slice_fusion, bf16[512,3072,1]{0,1,2:T(8,128)(2,1)} %bitcast.235, f32[512,128]{0,1:T(8,128)S(1)} %copy-done.7), kind=kOutput, calls=%fused_computation.25 | convolution fusion | flops 3222269952 | bytes 9715712 | tf_op jit(solution)/shard_map/tf,qfd->qtd/dot_general | solution.py:101
  300.5 110.8 %psum.7 = f32[8,32]{1,0:T(8,128)S(1)} all-reduce(f32[8,32]{1,0:T(8,128)S(1)} %fusion.39), channel_id=1, replica_groups=mesh['dp'=64,'owner'=8] {'dp','owner'}, use_global_device_ids=true, to_apply=%region_4.5 | all-reduce | flops 256 | bytes 2048 | tf_op jit(solution)/shard_map/psum | solution.py:136
  (60 shorter events, 14.8 us)
Async XLA Ops:
  6.5 12.3 %copy-start = (bf16[12,256,256]{2,1,0:T(8,128)(2,1)S(1)}, bf16[12,256,256]{2,1,0:T(8,128)(2,1)}, u32[]{:S(2)}) copy-start(bf16[12,256,256]{2,1,0:T(8,128)(2,1)} %param.12) | copy-start | bytes 4718596
  6.5 143.8 %all-gather.3.cloned.1.call-start = ((), (), s32[]{:S(2)}) async-start(), calls=%async_computation.2 | async-start | bytes 3194880 | tf_op jit(solution)/shard_map/all_gather | solution.py:129
  8.5 11.3 %copy-start.8 = (bf16[8,8192]{1,0:T(8,128)(2,1)S(1)}, bf16[8,8192]{1,0:T(8,128)(2,1)}, u32[]{:S(2)}) copy-start(bf16[8,8192]{1,0:T(8,128)(2,1)} %param.11) | copy-start | bytes 393220
  8.7 9.6 %collective-permute-start = (bf16[16,6,256]{2,1,0:T(8,128)(2,1)S(1)}, bf16[16,6,256]{2,1,0:T(8,128)(2,1)S(1)}, u32[]{:S(2)}, u32[]{:S(2)}) collective-permute-start(bf16[16,6,256]{2,1,0:T(8,128)(2,1)S(1)} %fusion.20), channel_id=1, source_target_pairs={{0,1},{1,0},{2,3},{3,2},{4,5},{5,4},{6,7},{7,6},{8,9},{9,8},{10,11... | collective-permute-start | bytes 147464 | tf_op jit(solution)/shard_map/ppermute | solution.py:13
  18.8 50.0 %copy-start.9 = (bf16[1,128,128]{2,1,0:T(8,128)(2,1)S(1)}, bf16[1,128,128]{2,1,0:T(8,128)(2,1)}, u32[]{:S(2)}) copy-start(bf16[1,128,128]{2,1,0:T(8,128)(2,1)} %param.13) | copy-start | bytes 98308
  47.9 20.9 %all-to-all-start = ((bf16[8,64,128]{2,0,1:T(8,128)(2,1)}), bf16[8,64,128]{2,0,1:T(8,128)(2,1)S(1)}, u32[]{:S(2)}, u32[]{:S(2)}) async-start(bf16[8,64,128]{2,0,1:T(8,128)(2,1)} %bitcast.12), calls=%async_computation | async-start | bytes 262144 | tf_op jit(solution)/shard_map/all_to_all | solution.py:118
  54.3 234.0 %all-gather.5.cloned.1.call-start = ((), (), s32[]{:S(2)}) async-start(), calls=%async_computation.3 | async-start | bytes 3194880 | tf_op jit(solution)/shard_map/all_gather | solution.py:131
  238.3 1.9 copy-start.1
  239.3 1.9 copy-start.2
  240.2 1.9 copy-start.3
  241.2 1.9 copy-start.4
  242.1 1.9 copy-start.5
  243.1 1.9 copy-start.6
  245.9 47.1 %copy-start.7 = (f32[512,128]{0,1:T(8,128)S(1)}, f32[512,128]{0,1:T(8,128)}, u32[]{:S(2)}) copy-start(f32[512,128]{0,1:T(8,128)} %copy.123) | copy-start | bytes 786436
Sparse Core Ops, SparseCore 0:
  19.9 130.3 all-gather.2
  153.2 135.1 all-gather.4
where the time goes:
time: 420 us; the launch traced here: 419 us
  blocking collectives  139 us (33%)
  waiting for transfers between devices  136 us (32%)
  local copies, waits for them, and re-layouts  58.8 us (14%)
  matrix products  53 us (13%)
  starting transfers between devices  15.4 us (4%)
  between operations  13.6 us (3%)
    psum x1, blocking collectives, local(): scores = lax.psum(partial_scores, ('dp', 'owner'))  111 us
    all_gather x1, waiting for transfers between devices, local(): query_all = lax.all_gather(query_rot, 'dp', axis=0, tiled=True)  80.6 us
    all_gather x1, waiting for transfers between devices, local(): piece_slots = lax.all_gather(train_local, 'dp', axis=0, tiled=True)  42.4 us
    all_to_all x1, blocking collectives, local(): lax.all_to_all(train_in, 'dp', split_axis=1, concat_axis=0, tiled=True)  28.1 us
    dot_general x8, matrix products, condition(): jnp.einsum('fnb,ncb->fnc', damped.reshape(-1, in_blocks, in_width), basis...  24.3 us
    dot_general x8, matrix products, condition(): jnp.einsum('ckl,cld->ckd', basis_out, half_back.reshape(capacity, block_w...  18.7 us
    another operation x9, local copies, waits for them, and re-layouts, condition(): return jnp.stack(results)  16.5 us
    convert_element_type x8, local copies, waits for them, and re-layouts, condition(): restored = jnp.einsum('ckl,cld->ckd', basis_out, half_back.reshape(capaci...  15.3 us
  transfers between devices with their start and end apart: 4, of which 4 were waited for; matrix products, arithmetic and copies ran while one was open for 24% of the time, Pallas kernels for 0%

commit v1 on v0

--- a/solution.py
+++ b/solution.py
@@ -133,7 +133,7 @@
     partial_scores = score_tokens(
         precond, piece_slots.reshape(row_count, -1), train_cols, example_count
     )
-    scores = lax.psum(partial_scores, ("dp", "owner"))
+    scores = lax.psum(lax.psum(partial_scores, "dp"), "owner")
     per_query = query_act.shape[0] // NQ
     hidden_total = query_out.shape[1] * lax.axis_size("owner")
     score_scale = 1.0 / math.sqrt(per_query * ET * hidden_total * query_in.shape[1])

time: 420 us -> 473 us (1.13)
  blocking collectives: 139 us -> 192 us
    psum x1 -> x2, blocking collectives: 111 us -> 163 us  [local(): scores = lax.psum(lax.psum(partial_scores, 'dp'), 'owner')]
  transfers between devices with their start and end apart: 4 -> 4, of which waited for: 4 -> 4; matrix products, arithmetic and copies ran while one was open for 24% -> 21% of each run, Pallas kernels for 0% -> 0%
where the time goes in v1:
time: 473 us; the launch traced here: 471 us
  blocking collectives  192 us (41%)
  waiting for transfers between devices  136 us (29%)
  local copies, waits for them, and re-layouts  58.6 us (12%)
  matrix products  53 us (11%)
  starting transfers between devices  15.4 us (3%)
  between operations  13.6 us (3%)
    psum x2, blocking collectives, local(): scores = lax.psum(lax.psum(partial_scores, 'dp'), 'owner')  163 us
    all_gather x1, waiting for transfers between devices, local(): query_all = lax.all_gather(query_rot, 'dp', axis=0, tiled=True)  80.6 us
    all_gather x1, waiting for transfers between devices, local(): piece_slots = lax.all_gather(train_local, 'dp', axis=0, tiled=True)  42.7 us
    all_to_all x1, blocking collectives, local(): lax.all_to_all(train_in, 'dp', split_axis=1, concat_axis=0, tiled=True)  28.1 us
    dot_general x8, matrix products, condition(): jnp.einsum('fnb,ncb->fnc', damped.reshape(-1, in_blocks, in_width), basis...  24.3 us
    dot_general x8, matrix products, condition(): jnp.einsum('ckl,cld->ckd', basis_out, half_back.reshape(capacity, block_w...  18.7 us
    another operation x9, local copies, waits for them, and re-layouts, condition(): return jnp.stack(results)  16.4 us
    convert_element_type x8, local copies, waits for them, and re-layouts, condition(): restored = jnp.einsum('ckl,cld->ckd', basis_out, half_back.reshape(capaci...  15.3 us
  transfers between devices with their start and end apart: 4, of which 4 were waited for; matrix products, arithmetic and copies ran while one was open for 21% of the time, Pallas kernels for 0%

profile of v1, /device:TPU:1, one launch (start us, length us, event | category | flops | bytes accessed | tf_op | source)
XLA Modules:
  0.0 471.4 jit_solution(7601752063701406957)
XLA Ops:
  8.7 8.7 %collective-permute-start = (bf16[16,6,256]{2,1,0:T(8,128)(2,1)S(1)}, bf16[16,6,256]{2,1,0:T(8,128)(2,1)S(1)}, u32[]{:S(2)}, u32[]{:S(2)}) collective-permute-start(bf16[16,6,256]{2,1,0:T(8,128)(2,1)S(1)} %fusion.20), channel_id=1, source_target_pairs={{0,1},{1,0},{2,3},{3,2},{4,5},{5,4},{6,7},{7,6},{8,9},{9,8},{10,11... | collective-permute-start | bytes 147464 | tf_op jit(solution)/shard_map/ppermute | solution.py:13
  19.8 28.1 %all_to_all.29 = bf16[8,64,128]{2,0,1:T(8,128)(2,1)S(1)} all-to-all(bf16[8,64,128]{2,0,1:T(8,128)(2,1)S(1)} %bitcast.263), channel_id=1, replica_groups=mesh['dp'=64,'owner'=8] {'dp'}, dimensions={1} | all-to-all | bytes 262144 | tf_op jit(solution)/shard_map/all_to_all | solution.py:119
  47.9 6.4 %all-to-all-start = ((bf16[8,64,128]{2,0,1:T(8,128)(2,1)}), bf16[8,64,128]{2,0,1:T(8,128)(2,1)S(1)}, u32[]{:S(2)}, u32[]{:S(2)}) async-start(bf16[8,64,128]{2,0,1:T(8,128)(2,1)} %bitcast.12), calls=%async_computation | async-start | bytes 262144 | tf_op jit(solution)/shard_map/all_to_all | solution.py:118
  56.1 12.7 %all-to-all-done = bf16[8,64,128]{2,0,1:T(8,128)(2,1)S(1)} async-done(((bf16[8,64,128]{2,0,1:T(8,128)(2,1)}), bf16[8,64,128]{2,0,1:T(8,128)(2,1)S(1)}, u32[]{:S(2)}, u32[]{:S(2)}) %all-to-all-start) | async-done | bytes 131104 | tf_op jit(solution)/shard_map/all_to_all | solution.py:118
  69.7 80.6 %all-gather.3.cloned.1.call-done = bf16[512,12,256]{2,0,1:T(8,128)(2,1)} async-done(((bf16[8,12,256]{2,0,1:T(8,128)(2,1)}), bf16[512,12,256]{2,0,1:T(8,128)(2,1)}) %all-gather.3.cloned.1.call-update) | async-done | bytes 3145744 | tf_op jit(solution)/shard_map/all_gather | solution.py:129
  150.3 3.3 slice_bitcast_fusion
  153.7 2.1 convolution_convert_fusion.7
  157.1 1.0 copy.135
  158.1 3.1 convolution_convert_fusion.6
  161.2 1.8 fusion.10
  163.0 1.2 copy.93
  164.1 1.4 copy.113
  165.6 1.8 copy.136
  167.3 3.2 convolution_convert_fusion.5
  170.5 2.7 fusion.11
  173.2 2.3 copy.96
  175.5 2.3 copy.114
  177.7 1.8 copy.137
  179.5 3.2 convolution_convert_fusion.4
  182.7 2.7 fusion.12
  185.4 2.3 copy.99
  187.7 2.3 copy.115
  190.0 1.8 copy.138
  191.8 3.2 convolution_convert_fusion.3
  195.0 2.7 fusion.13
  197.6 2.3 copy.102
  199.9 2.3 copy.116
  202.2 1.8 copy.139
  204.0 3.2 convolution_convert_fusion.2
  207.2 2.7 fusion.14
  209.9 2.3 copy.105
  212.2 2.3 copy.117
  214.5 1.8 copy.140
  216.2 3.2 convolution_convert_fusion.1
  219.4 2.9 fusion.15
  222.3 2.3 copy.108
  224.6 2.3 copy.118
  227.7 3.2 convolution_convert_fusion
  230.9 2.7 fusion.16
  233.6 2.3 copy.111
  235.8 2.3 copy.119
  240.0 1.0 constant_dynamic-update-slice_fusion.5
  241.0 0.9 constant_dynamic-update-slice_fusion.4
  245.7 42.7 %all-gather.5.cloned.1.call-done = bf16[512,12,256]{2,0,1:T(8,128)(2,1)} async-done(((bf16[8,12,256]{2,0,1:T(8,128)(2,1)}), bf16[512,12,256]{2,0,1:T(8,128)(2,1)}) %all-gather.5.cloned.1.call-update) | async-done | bytes 3145744 | tf_op jit(solution)/shard_map/all_gather | solution.py:131
  288.4 4.7 copy.121
  293.1 7.1 %fusion.8 = f32[8,512]{1,0:T(8,128)S(1)} fusion(bf16[8,3072,128]{1,2,0:T(8,128)(2,1)} %constant_dynamic-update-slice_fusion, bf16[512,3072,1]{0,1,2:T(8,128)(2,1)} %bitcast.235, f32[512,128]{0,1:T(8,128)S(1)} %copy-done.7), kind=kOutput, calls=%fused_computation.25 | convolution fusion | flops 3222269952 | bytes 9715712 | tf_op jit(solution)/shard_map/tf,qfd->qtd/dot_general | solution.py:101
  300.5 113.0 %psum.14 = f32[8,32]{1,0:T(8,128)S(1)} all-reduce(f32[8,32]{1,0:T(8,128)S(1)} %fusion.39), channel_id=1, replica_groups=mesh['dp'=64,'owner'=8] {'dp'}, use_global_device_ids=true, to_apply=%region_4.5 | all-reduce | flops 256 | bytes 2048 | tf_op jit(solution)/shard_map/psum | solution.py:136
  413.4 50.5 %psum.15 = f32[8,32]{1,0:T(8,128)S(1)} all-reduce(f32[8,32]{1,0:T(8,128)S(1)} %psum.14), channel_id=1, replica_groups=mesh['dp'=64,'owner'=8] {'owner'}, use_global_device_ids=true, to_apply=%region_5.6 | all-reduce | flops 256 | bytes 2048 | tf_op jit(solution)/shard_map/psum | solution.py:136
  (61 shorter events, 15.7 us)
Async XLA Ops:
  6.5 12.3 %copy-start = (bf16[12,256,256]{2,1,0:T(8,128)(2,1)S(1)}, bf16[12,256,256]{2,1,0:T(8,128)(2,1)}, u32[]{:S(2)}) copy-start(bf16[12,256,256]{2,1,0:T(8,128)(2,1)} %param.12) | copy-start | bytes 4718596
  6.5 143.8 %all-gather.3.cloned.1.call-start = ((), (), s32[]{:S(2)}) async-start(), calls=%async_computation.2 | async-start | bytes 3194880 | tf_op jit(solution)/shard_map/all_gather | solution.py:129
  8.5 11.3 %copy-start.8 = (bf16[8,8192]{1,0:T(8,128)(2,1)S(1)}, bf16[8,8192]{1,0:T(8,128)(2,1)}, u32[]{:S(2)}) copy-start(bf16[8,8192]{1,0:T(8,128)(2,1)} %param.11) | copy-start | bytes 393220
  8.7 9.6 %collective-permute-start = (bf16[16,6,256]{2,1,0:T(8,128)(2,1)S(1)}, bf16[16,6,256]{2,1,0:T(8,128)(2,1)S(1)}, u32[]{:S(2)}, u32[]{:S(2)}) collective-permute-start(bf16[16,6,256]{2,1,0:T(8,128)(2,1)S(1)} %fusion.20), channel_id=1, source_target_pairs={{0,1},{1,0},{2,3},{3,2},{4,5},{5,4},{6,7},{7,6},{8,9},{9,8},{10,11... | collective-permute-start | bytes 147464 | tf_op jit(solution)/shard_map/ppermute | solution.py:13
  18.8 50.0 %copy-start.9 = (bf16[1,128,128]{2,1,0:T(8,128)(2,1)S(1)}, bf16[1,128,128]{2,1,0:T(8,128)(2,1)}, u32[]{:S(2)}) copy-start(bf16[1,128,128]{2,1,0:T(8,128)(2,1)} %param.13) | copy-start | bytes 98308
  47.9 20.9 %all-to-all-start = ((bf16[8,64,128]{2,0,1:T(8,128)(2,1)}), bf16[8,64,128]{2,0,1:T(8,128)(2,1)S(1)}, u32[]{:S(2)}, u32[]{:S(2)}) async-start(bf16[8,64,128]{2,0,1:T(8,128)(2,1)} %bitcast.12), calls=%async_computation | async-start | bytes 262144 | tf_op jit(solution)/shard_map/all_to_all | solution.py:118
  54.3 234.0 %all-gather.5.cloned.1.call-start = ((), (), s32[]{:S(2)}) async-start(), calls=%async_computation.3 | async-start | bytes 3194880 | tf_op jit(solution)/shard_map/all_gather | solution.py:131
  238.1 1.9 copy-start.1
  239.1 1.9 copy-start.2
  240.0 1.9 copy-start.3
  241.0 1.9 copy-start.4
  241.9 1.9 copy-start.5
  242.9 1.9 copy-start.6
  245.7 47.3 %copy-start.7 = (f32[512,128]{0,1:T(8,128)S(1)}, f32[512,128]{0,1:T(8,128)}, u32[]{:S(2)}) copy-start(f32[512,128]{0,1:T(8,128)} %copy.123) | copy-start | bytes 786436
Sparse Core Ops, SparseCore 0:
  19.9 130.3 all-gather.2
  153.2 135.1 all-gather.4
